TPU v7x, 32 devices: a whole 2x2x4 slice. The times are simulated.
32 devices in a mesh: prow: 8 (over z, x), pcol: 4 (over y, core).
Axes of the slice: x: 2, y: 2, z: 4, core: 2. Of those that a mesh axis runs over, the one named last changes fastest.
Arguments:
- sigma_top: bfloat16 [8, 8, 128, 128], P('prow', 'pcol'), may hold values from -6 to 6
- factor_one: bfloat16 [8, 8, 128, 128], P('prow', 'pcol'), may hold values from -0.1875 to 0.1875
- inverse_one: bfloat16 [8, 128, 128], P('prow'), may hold values from -0.5 to 0.5
- pattern_one: int32 [8, 8], replicated, may hold values from 0 to 7, as said below
- factor_two: bfloat16 [8, 8, 128, 128], P('prow', 'pcol'), may hold values from -0.25 to 0.25
- parent_block: bfloat16 [8, 128, 128], P('prow'), may hold values from -0.25 to 0.25
- inverse_two: bfloat16 [8, 128, 128], P('prow'), may hold values from -0.5 to 0.5
- parent_two: int32 [8], replicated, may hold values from 0 to 7
- keep_two: int32 [8, 8], replicated, may hold values 0 or 1
Outputs:
- inverse_top_one: bfloat16 [8, 8, 128, 128], P('prow')
- diag_one: float32 [8, 128, 128], P('prow')
- inverse_top_two: bfloat16 [8, 8, 128, 128], P('prow')
- inverse_parent_two: float32 [8, 128, 128], P('prow')
- diag_two: float32 [8, 128, 128], P('prow')
Inputs may be any that keep to these rules, and one draw needn't show every extreme that they name: Each row of pattern_one lists 8 distinct block rows of the top region. keep_two[i, k] = 1 where level-two supernode i's pattern holds the k-th tile of its parent's pattern. parent_two names level-one supernodes.
All inputs are finite; a program needn't handle non-finite values.
Results may differ from a plain program's by a relative error of at most 0.023.
Values may be sent and summed in bfloat16 or wider, within the bound.
A program may use at most 64 MiB of HBM per device.

v0:
```python
import jax
import jax.numpy as jnp
from jax import lax
from jax.sharding import PartitionSpec as P

highest = lax.Precision.HIGHEST


def split_product(form, left, right):
    upper_part = right.astype(jnp.bfloat16)
    lower_part = (right - upper_part.astype(jnp.float32)).astype(jnp.bfloat16)
    first = jnp.einsum(form, left, upper_part, preferred_element_type=jnp.float32)
    return first + jnp.einsum(form, left, lower_part, preferred_element_type=jnp.float32)


def body(
    sigma_top,
    factor_one,
    inverse_one,
    pattern_one,
    factor_two,
    parent_block,
    inverse_two,
    parent_two,
    keep_two,
):
    rows_here = sigma_top.shape[0]
    cols_here = sigma_top.shape[1]
    tile_width = sigma_top.shape[2]
    prow_index = lax.axis_index("prow")
    pcol_index = lax.axis_index("pcol")
    first_row = prow_index * rows_here
    column_ids = pcol_index * cols_here + jnp.arange(cols_here, dtype=jnp.int32)
    top_rows = first_row + jnp.arange(rows_here, dtype=jnp.int32)
    owner_column = first_row // cols_here
    diagonal_owner = owner_column == pcol_index
    offset = jnp.clip(first_row - pcol_index * cols_here, 0, cols_here - rows_here)
    total_one = pattern_one.shape[0]
    local_one = factor_one.shape[0]
    lower_one = jnp.tril(inverse_one)
    scaled_local = jnp.einsum(
        "jkwv,jvx->jkwx", factor_one, lower_one, preferred_element_type=jnp.float32
    ).astype(jnp.bfloat16)
    scaled_rows = lax.all_gather(scaled_local, "pcol", axis=1, tiled=True)
    own_pattern = lax.dynamic_slice_in_dim(pattern_one, prow_index * local_one, local_one, 0)
    picker_one = (own_pattern[:, :, None] == column_ids[None, None, :]).astype(jnp.bfloat16)
    spread_one = jnp.einsum(
        "jkc,jkwv->jcwv", picker_one, scaled_rows, preferred_element_type=jnp.float32
    ).astype(jnp.bfloat16)
    spread_all = lax.all_gather(spread_one, "prow", axis=0, tiled=True)
    partial_one = jnp.einsum(
        "acwv,jcvx->ajwx", sigma_top, spread_all, preferred_element_type=jnp.float32
    )
    summed_one = lax.psum(partial_one.astype(jnp.bfloat16), "pcol").astype(jnp.float32)
    member_one = jnp.sum(
        (pattern_one[None, :, :] == top_rows[:, None, None]).astype(jnp.float32), axis=2
    )
    inverse_top_one = (-summed_one * member_one[:, :, None, None]).astype(jnp.bfloat16)
    own_rows = lax.dynamic_slice_in_dim(spread_all, offset, rows_here, 1)
    quadratic_one = split_product("jawv,ajwx->jvx", own_rows, summed_one)
    quadratic_one = jnp.where(diagonal_owner, quadratic_one, 0.0)
    lower_float = lower_one.astype(jnp.float32)
    gram_one = jnp.einsum("jwv,jwx->jvx", lower_float, lower_float, precision=highest)
    placed = lax.dynamic_update_slice_in_dim(
        jnp.zeros((total_one, tile_width, tile_width), jnp.float32),
        gram_one,
        prow_index * local_one,
        0,
    )
    partial_diag = quadratic_one + jnp.where(pcol_index == 0, placed, 0.0)
    diagonal_all = lax.psum(partial_diag, ("prow", "pcol"))
    diag_one = lax.dynamic_slice_in_dim(diagonal_all, prow_index * local_one, local_one, 0)
    local_two = factor_two.shape[0]
    lower_two = jnp.tril(inverse_two)
    scaled_two = jnp.einsum(
        "ikwv,ivx->ikwx", factor_two, lower_two, preferred_element_type=jnp.float32
    ).astype(jnp.bfloat16)
    scaled_parent = jnp.einsum(
        "iwv,ivx->iwx", parent_block, lower_two, preferred_element_type=jnp.float32
    ).astype(jnp.bfloat16)
    scaled_rows_two = lax.all_gather(scaled_two, "pcol", axis=1, tiled=True)
    parent_hot = (parent_two[:, None] == jnp.arange(total_one, dtype=jnp.int32)[None, :]).astype(
        jnp.int32
    )
    parent_pattern = jnp.sum(parent_hot[:, :, None] * pattern_one[None, :, :], axis=1)
    own_parent_pattern = lax.dynamic_slice_in_dim(
        parent_pattern, prow_index * local_two, local_two, 0
    )
    own_keep = lax.dynamic_slice_in_dim(keep_two, prow_index * local_two, local_two, 0)
    picker_two = (
        (own_parent_pattern[:, :, None] == column_ids[None, None, :]).astype(jnp.int32)
        * own_keep[:, :, None]
    ).astype(jnp.bfloat16)
    spread_two = jnp.einsum(
        "ikc,ikwv->icwv", picker_two, scaled_rows_two, preferred_element_type=jnp.float32
    ).astype(jnp.bfloat16)
    spread_all_two, parent_all = (
        lax.all_gather(spread_two, "prow", axis=0, tiled=True),
        lax.all_gather(scaled_parent, "prow", axis=0, tiled=True),
    )
    partial_two = jnp.einsum(
        "acwv,icvx->aiwx", sigma_top, spread_all_two, preferred_element_type=jnp.float32
    )
    inherited = jnp.einsum(
        "ij,ajwv->aiwv",
        parent_hot.astype(jnp.bfloat16),
        inverse_top_one,
        preferred_element_type=jnp.float32,
    ).astype(jnp.bfloat16)
    carried_rows = jnp.einsum(
        "aiwv,ivx->aiwx", inherited, parent_all, preferred_element_type=jnp.float32
    )
    partial_two = partial_two + jnp.where(diagonal_owner, carried_rows, 0.0)
    summed_two = lax.psum(partial_two.astype(jnp.bfloat16), "pcol").astype(jnp.float32)
    member_two = jnp.sum(
        (parent_pattern[None, :, :] == top_rows[:, None, None]).astype(jnp.float32)
        * keep_two[None, :, :].astype(jnp.float32),
        axis=2,
    )
    inverse_top_two = (-summed_two * member_two[:, :, None, None]).astype(jnp.bfloat16)
    own_two = lax.dynamic_slice_in_dim(spread_all_two, offset, rows_here, 1)
    cross = jnp.einsum("aiwv,iawx->ivx", inherited, own_two, preferred_element_type=jnp.float32)
    quadratic_two = split_product("iawv,aiwx->ivx", own_two, summed_two)
    cross = jnp.where(diagonal_owner, cross, 0.0)
    quadratic_two = jnp.where(diagonal_owner, quadratic_two, 0.0)
    cross_part, quadratic_part = (
        lax.psum_scatter(
            cross.astype(jnp.bfloat16), "prow", scatter_dimension=0, tiled=True
        ).astype(jnp.float32),
        lax.psum_scatter(
            quadratic_two.astype(jnp.bfloat16), "prow", scatter_dimension=0, tiled=True
        ).astype(jnp.float32),
    )
    cross_sum, quadratic_sum = (
        lax.psum(cross_part.astype(jnp.bfloat16), "pcol").astype(jnp.float32),
        lax.psum(quadratic_part.astype(jnp.bfloat16), "pcol").astype(jnp.float32),
    )
    own_hot = lax.dynamic_slice_in_dim(parent_hot, prow_index * local_two, local_two, 0).astype(
        jnp.float32
    )
    parent_diag = jnp.einsum("ij,jwv->iwv", own_hot, diagonal_all, precision=highest)
    parent_float = scaled_parent.astype(jnp.float32)
    carried = cross_sum + jnp.einsum("iwv,ivx->iwx", parent_diag, parent_float, precision=highest)
    lower_two_float = lower_two.astype(jnp.float32)
    diag_two = jnp.einsum("iwv,iwx->ivx", lower_two_float, lower_two_float, precision=highest)
    diag_two = (
        diag_two
        + quadratic_sum
        + jnp.einsum("iwv,iwx->ivx", parent_float, carried, precision=highest)
    )
    return (inverse_top_one, diag_one, inverse_top_two, -carried, diag_two)


def solution(mesh):
    in_specs = (
        P("prow", "pcol", None, None),
        P("prow", "pcol", None, None),
        P("prow", None, None),
        P(),
        P("prow", "pcol", None, None),
        P("prow", None, None),
        P("prow", None, None),
        P(),
        P(),
    )
    out_specs = (
        P("prow", None, None, None),
        P("prow", None, None),
        P("prow", None, None, None),
        P("prow", None, None),
        P("prow", None, None),
    )
    return jax.shard_map(body, mesh=mesh, in_specs=in_specs, out_specs=out_specs, check_vma=False)
```

profile of v0, /device:TPU:0, one launch (start us, length us, event | category | flops | bytes accessed | tf_op | source)
XLA Modules:
  0.0 453.0 jit_solution(8151209483114322396)
XLA Ops:
  7.2 1.1 fusion.10
  8.4 7.2 %all-gather = bf16[8,128,128]{2,1,0:T(8,128)(2,1)S(1)} all-gather(bf16[2,128,128]{2,1,0:T(8,128)(2,1)S(1)} %copy.72), channel_id=2, replica_groups=mesh['prow'=8,'pcol'=4] {'pcol'}, dimensions={0}, use_global_device_ids=true | all-gather | bytes 327680 | tf_op jit(solution)/shard_map/all_gather | solution.py:44
  16.0 31.9 %all-gather.1 = bf16[16,128,128]{2,1,0:T(8,128)(2,1)S(1)} all-gather(bf16[2,128,128]{2,1,0:T(8,128)(2,1)S(1)} %copy.74), channel_id=3, replica_groups=mesh['prow'=8,'pcol'=4] {'prow'}, dimensions={0}, use_global_device_ids=true | all-gather | bytes 589824 | tf_op jit(solution)/shard_map/all_gather | solution.py:50
  47.9 1.1 fusion.7
  49.5 0.3 copy-done.11
  50.0 0.6 copy-done.10
  50.9 5.8 %all-gather.2 = bf16[8,128,128]{2,1,0:T(8,128)(2,1)S(1)} all-gather(bf16[2,128,128]{2,1,0:T(8,128)(2,1)S(1)} %copy.79), channel_id=4, replica_groups=mesh['prow'=8,'pcol'=4] {'pcol'}, dimensions={0}, use_global_device_ids=true | all-gather | bytes 327680 | tf_op jit(solution)/shard_map/all_gather | solution.py:81
  57.0 31.5 %all-gather.3 = bf16[16,128,128]{2,1,0:T(8,128)(2,1)S(1)} all-gather(bf16[2,128,128]{2,1,0:T(8,128)(2,1)S(1)} %copy.81), channel_id=5, replica_groups=mesh['prow'=8,'pcol'=4] {'prow'}, dimensions={0}, use_global_device_ids=true | all-gather | bytes 589824 | tf_op jit(solution)/shard_map/all_gather | solution.py:98
  88.7 26.4 %all-gather.4 = bf16[1024,128]{0,1:T(8,128)(2,1)S(1)} all-gather(bf16[128,128]{0,1:T(8,128)(2,1)S(1)} %bitcast.162), channel_id=6, replica_groups=mesh['prow'=8,'pcol'=4] {'prow'}, dimensions={0}, use_global_device_ids=true | all-gather | bytes 294912 | tf_op jit(solution)/shard_map/all_gather | solution.py:99
  115.1 0.3 convolution_bitcast_fusion
  115.5 1.1 fusion.112
  117.2 0.9 fusion.9
  118.2 0.9 copy-done.1
  119.1 0.3 fusion.37
  119.4 0.3 fusion.2
  119.7 0.4 copy-done.5
  120.4 0.8 copy-done.2
  121.5 1.0 fusion.6
  122.7 26.8 %all-reduce.10.cloned.1.call-done = bf16[1,8,128,128]{2,3,1,0:T(8,128)(2,1)} async-done(((bf16[1,8,128,128]{2,3,1,0:T(8,128)(2,1)}), bf16[1,8,128,128]{2,3,1,0:T(8,128)(2,1)}) %all-reduce.10.cloned.1.call-update) | async-done | bytes 262160 | tf_op jit(solution)/shard_map/psum | solution.py:114
  149.5 1.3 fusion.32
  150.9 1.0 fusion.3
  152.1 0.9 copy.92
  153.0 0.9 copy.93
  153.9 128.7 %all-reduce.8.cloned.1.call-done = f32[8,128,128]{2,1,0:T(8,128)} async-done(((f32[8,128,128]{2,1,0:T(8,128)}), f32[8,128,128]{2,1,0:T(8,128)}) %all-reduce.8.cloned.1.call-update) | async-done | bytes 524304 | tf_op jit(solution)/shard_map/psum | solution.py:71
  282.6 1.8 fusion.24
  284.5 61.9 %reduce-scatter.3.cloned.1.call-done = bf16[1,128,128]{2,1,0:T(8,128)(2,1)} async-done(((bf16[8,128,128]{2,1,0:T(8,128)(2,1)}), bf16[1,128,128]{2,1,0:T(8,128)(2,1)}) %reduce-scatter.3.cloned.1.call-update) | async-done | bytes 32784 | tf_op jit(solution)/shard_map/reduce_scatter | solution.py:127
  346.4 63.8 %reduce-scatter.5.cloned.1.call-done = bf16[1,128,128]{2,1,0:T(8,128)(2,1)} async-done(((bf16[8,128,128]{2,1,0:T(8,128)(2,1)}), bf16[1,128,128]{2,1,0:T(8,128)(2,1)}) %reduce-scatter.5.cloned.1.call-update) | async-done | bytes 32784 | tf_op jit(solution)/shard_map/reduce_scatter | solution.py:130
  410.3 1.5 constant_dynamic-slice_fusion.3
  411.8 31.2 %all-reduce.12.cloned.1.call-done = (bf16[1,128,128]{2,1,0:T(8,128)(2,1)}, bf16[1,128,128]{2,1,0:T(8,128)(2,1)}) async-done(((bf16[1,128,128]{2,1,0:T(8,128)(2,1)}, bf16[1,128,128]{2,1,0:T(8,128)(2,1)}), (bf16[1,128,128]{2,1,0:T(8,128)(2,1)}, bf16[1,128,128]{2,1,0:T(8,128)(2,1)})) %all-reduce.12.cloned.1.call-update) | async-done | bytes 65552 | tf_op jit(solution)/shard_map/psum | solution.py:135
  442.9 1.6 fusion.102
  444.7 0.6 copy-done.8
  445.3 0.8 fusion.15
  (56 shorter events, 3.9 us)
Async XLA Ops:
  7.2 40.7 %copy-start = (bf16[1,2,128,128]{3,2,1,0:T(8,128)(2,1)S(1)}, bf16[1,2,128,128]{3,2,1,0:T(8,128)(2,1)}, u32[]{:S(2)}) copy-start(bf16[1,2,128,128]{3,2,1,0:T(8,128)(2,1)} %param.9) | copy-start | bytes 196612
  7.2 108.3 %all-reduce.6.cloned.1.call-start = ((), (), s32[]{:S(2)}) async-start(), calls=%async_computation.2 | async-start | bytes 524288 | tf_op jit(solution)/shard_map/psum | solution.py:54
  8.4 7.2 %copy-start.9 = (s32[8,8]{1,0:T(8,128)S(1)}, s32[8,8]{1,0:T(8,128)}, u32[]{:S(2)}) copy-start(s32[8,8]{1,0:T(8,128)} %param.12) | copy-start | bytes 772
  48.9 100.6 %all-reduce.10.cloned.1.call-start = ((), (), s32[]{:S(2)}) async-start(), calls=%async_computation.4 | async-start | bytes 524288 | tf_op jit(solution)/shard_map/psum | solution.py:114
  49.1 0.7 copy-start.11
  49.1 1.4 copy-start.6
  49.4 1.1 copy-start.4
  49.8 0.7 copy-start.10
  57.0 31.5 %copy-start.7 = (bf16[1,128,128]{2,1,0:T(8,128)(2,1)S(1)}, bf16[1,128,128]{2,1,0:T(8,128)(2,1)}, u32[]{:S(2)}) copy-start(bf16[1,128,128]{2,1,0:T(8,128)(2,1)} %param.14) | copy-start | bytes 98308
  118.2 0.9 copy-start.1
  118.2 164.4 %all-reduce.8.cloned.1.call-start = ((), (), s32[]{:S(2)}) async-start(), calls=%async_computation.3 | async-start | bytes 1048576 | tf_op jit(solution)/shard_map/psum | solution.py:71
  119.4 0.8 copy-start.5
  120.4 0.8 copy-start.2
  121.2 225.2 %reduce-scatter.3.cloned.1.call-start = ((), (), s32[]{:S(2)}) async-start(), calls=%async_computation.5 | async-start | bytes 294912 | tf_op jit(solution)/shard_map/reduce_scatter | solution.py:127
  122.6 287.7 %reduce-scatter.5.cloned.1.call-start = ((), (), s32[]{:S(2)}) async-start(), calls=%async_computation.6 | async-start | bytes 294912 | tf_op jit(solution)/shard_map/reduce_scatter | solution.py:130
  149.5 1.3 copy-start.3
  151.9 291.0 %all-reduce.12.cloned.1.call-start = ((), (), s32[]{:S(2)}) async-start(), calls=%async_computation.7 | async-start | bytes 131072 | tf_op jit(solution)/shard_map/psum | solution.py:135
  444.5 0.8 copy-start.8
Sparse Core Ops, SparseCore 0:
  49.1 32.7 all-reduce.5
  118.3 31.1 all-reduce.9
  154.8 127.7 all-reduce.7
  286.2 60.2 reduce-scatter.2
  350.0 60.2 reduce-scatter.4
  412.6 30.2 all-reduce.11
where the time goes:
time: 454 us; the launch traced here: 453 us
  waiting for transfers between devices  313 us (69%)
  blocking collectives  103 us (23%)
  between operations  14.4 us (3%)
  matrix products  13.2 us (3%)
  local copies, waits for them, and re-layouts  8.08 us (2%)
    psum x1, waiting for transfers between devices, body(): diagonal_all = lax.psum(partial_diag, ('prow', 'pcol'))  129 us
    reduce_scatter x1, waiting for transfers between devices, body(): lax.psum_scatter(quadratic_two.astype(jnp.bfloat16), 'prow', scatter_dime...  63.8 us
    reduce_scatter x1, waiting for transfers between devices, body(): lax.psum_scatter(cross.astype(jnp.bfloat16), 'prow', scatter_dimension=0,...  61.9 us
    all_gather x1, blocking collectives, body(): spread_all = lax.all_gather(spread_one, 'prow', axis=0, tiled=True)  31.9 us
    all_gather x1, blocking collectives, body(): lax.all_gather(spread_two, 'prow', axis=0, tiled=True)  31.5 us
    psum x1, waiting for transfers between devices, body(): lax.psum(cross_part.astype(jnp.bfloat16), 'pcol').astype(jnp.float32)  31.2 us
    psum x1, waiting for transfers between devices, body(): lax.psum(partial_two.astype(jnp.bfloat16), 'pcol').astype(jnp.float32)  26.8 us
    all_gather x1, blocking collectives, body(): lax.all_gather(scaled_parent, 'prow', axis=0, tiled=True)  26.4 us
  transfers between devices with their start and end apart: 6, of which 5 were waited for; matrix products, arithmetic and copies ran while one was open for 3% of the time, Pallas kernels for 0%

commit v1 on v0

v1 whole, which is shorter than its diff:
```python
import functools

import jax
import jax.numpy as jnp
from jax import lax
from jax.experimental import pallas as pl
from jax.experimental.pallas import tpu as pltpu
from jax.sharding import PartitionSpec as P

MESH = pl.DeviceIdType.MESH
f32 = jnp.float32
bf16 = jnp.bfloat16


def each(count, step, start=0):
    if count - start <= 8:
        for i in range(start, count):
            step(i)
    else:
        lax.fori_loop(start, count, lambda i, carry: (step(i), carry)[1], 0)


def dot(left, right):
    return jnp.dot(left, right, preferred_element_type=f32)


def dot_t(left, right):
    return dot(left.astype(f32).T.astype(bf16), right)


def kernel(
    prows, pcols, group,
    sigma, factor_one, inverse_one, factor_two, parent_block, inverse_two,
    pattern, parent, keep,
    top_one, diag_one, top_two, parent_out, diag_two,
    msg, par_msg, rx, par_rx, sig, spread, total, ag, two_send, two_recv, z_one, z_two, zr_one, zr_two, fin,
    msg_s, par_s, msg_r, par_r, sig_s, sig_r, ag_s, ag_r, two_s, two_r, z_s, zr_one_r, zr_two_r, fin_s, fin_r,
):
    planes = prows // group
    half = pcols // 2
    cols = sigma.shape[1]
    w = sigma.shape[2]
    tiles = factor_one.shape[1]
    reach = pattern.shape[1]
    tops = prows
    members = group * pcols
    slice_rows = w // pcols

    p = lax.axis_index("prow")
    c = lax.axis_index("pcol")
    z, x = p // group, p % group
    m = x * pcols + c
    home = c // 2 + (c % 2) * half
    j = home * group + x
    mine = p == j
    target_col = (z % half) * 2 + z // half

    def place(row):
        plane = row // group
        return (row % group) * pcols + (plane % half) * 2 + plane // half

    def peer(t):
        q = (m + t) % members
        return q, (z * group + q // pcols, q % pcols)

    barrier = pltpu.get_barrier_semaphore()

    def greet_plane(t):
        pl.semaphore_signal(barrier, inc=1, device_id=peer(t)[1], device_id_type=MESH)

    def greet_line(t):
        other = (z + 1 + t // pcols) % planes
        pl.semaphore_signal(
            barrier, inc=1, device_id=(other * group + x, t % pcols), device_id_type=MESH
        )

    each((planes - 1) * pcols, greet_line)
    each(members, greet_plane, 1)

    keep_lower = lax.broadcasted_iota(jnp.int32, (w, w), 0) >= lax.broadcasted_iota(
        jnp.int32, (w, w), 1
    )
    lower_one = jnp.where(keep_lower, inverse_one[0].astype(f32), 0.0).astype(bf16)
    lower_two = jnp.where(keep_lower, inverse_two[0].astype(f32), 0.0).astype(bf16)
    for k in range(tiles):
        msg[k] = dot(factor_one[0, k], lower_one).astype(bf16)
        msg[tiles + k] = dot(factor_two[0, k], lower_two).astype(bf16)
    part = parent_block[0, pl.ds(pl.multiple_of(c * slice_rows, slice_rows), slice_rows), :]
    par_msg[...] = dot(part, lower_two).astype(bf16)
    own_cols = pl.ds(c * cols, cols)
    sig[x, own_cols] = sigma[0]

    pl.semaphore_wait(barrier, (planes - 1) * pcols + members - 1)

    def msg_copy(t):
        other = (z + t) % planes
        return pltpu.make_async_remote_copy(
            src_ref=msg, dst_ref=rx.at[c], send_sem=msg_s.at[t], recv_sem=msg_r.at[c],
            device_id=(other * group + x, target_col), device_id_type=MESH,
        )

    def par_copy(t):
        other = (z + t) % planes
        return pltpu.make_async_remote_copy(
            src_ref=par_msg, dst_ref=par_rx.at[c], send_sem=par_s.at[t], recv_sem=par_r.at[c],
            device_id=(other * group + x, target_col), device_id_type=MESH,
        )

    stays = target_col == c
    for copy_to in (msg_copy, par_copy):
        each(planes, lambda t: copy_to(planes - t).start(), 1)

    @pl.when(jnp.logical_not(stays))
    def _():
        msg_copy(0).start()
        par_copy(0).start()

    @pl.when(stays)
    def _():
        pltpu.make_async_copy(msg, rx.at[c], msg_r.at[c]).start()
        pltpu.make_async_copy(par_msg, par_rx.at[c], par_r.at[c]).start()

    def sig_copy(t):
        return pltpu.make_async_remote_copy(
            src_ref=sigma.at[0], dst_ref=sig.at[x, own_cols], send_sem=sig_s.at[t],
            recv_sem=sig_r.at[m], device_id=peer(t)[1], device_id_type=MESH,
        )

    each(members, lambda t: sig_copy(t).start(), 1)

    def gram(lower):
        return jnp.where(mine, dot_t(lower, lower), 0.0)

    gram_one = gram(lower_one)
    gram_two = gram(lower_two)

    each(pcols, lambda t: pltpu.make_async_copy(rx.at[t], rx.at[t], msg_r.at[t]).wait())
    each(pcols, lambda t: pltpu.make_async_copy(par_rx.at[t], par_rx.at[t], par_r.at[t]).wait())

    up = parent[j]
    rows_one = [pattern[j, k] for k in range(reach)]
    rows_two = [pattern[up, k] for k in range(reach)]
    kept = [keep[j, k] for k in range(reach)]

    def find(rows, weights, b):
        column = tile = hit = jnp.int32(0)
        for k in range(reach):
            same = rows[k] == b
            if weights is not None:
                same = jnp.logical_and(same, weights[k] == 1)
            column = jnp.where(same, k // tiles, column)
            tile = jnp.where(same, k % tiles, tile)
            hit = jnp.where(same, 1, hit)
        return column, tile, hit.astype(f32)

    def fill(b):
        rows = pl.ds(pl.multiple_of(b * w, w), w)
        column, tile, hit = find(rows_one, None, b)
        spread[rows, 0:w] = (rx[column, tile].astype(f32) * hit).astype(bf16)
        column, tile, hit = find(rows_two, kept, b)
        spread[rows, w:2 * w] = (rx[column, tiles + tile].astype(f32) * hit).astype(bf16)

    each(tops, fill)
    scaled_parent = jnp.concatenate(
        [par_rx[t] for t in range(pcols)], axis=0
    )

    def sig_wait(t):
        q, _ = peer(t)
        ref = sig.at[q // pcols, pl.ds((q % pcols) * cols, cols)]
        pltpu.make_async_copy(ref, ref, sig_r.at[q]).wait()

    each(members, sig_wait, 1)

    chunk = 8 if tops % 8 == 0 else 1

    def product(b0):
        return [
            dot(
                jnp.concatenate([sig[g, b0 + b] for b in range(chunk)], axis=1),
                spread[pl.ds(pl.multiple_of(b0 * w, w), chunk * w), :],
            )
            for g in range(group)
        ]

    if tops == chunk:
        sums = product(0)
    else:
        total[...] = jnp.zeros_like(total)

        def add(n):
            for g, value in enumerate(product(n * chunk)):
                total[g] += value

        lax.fori_loop(0, tops // chunk, lambda n, carry: (add(n), carry)[1], 0)
        sums = [total[g] for g in range(group)]

    hits_one = [find(rows_one, None, z * group + g)[2] for g in range(group)]
    hits_two = [find(rows_two, kept, z * group + g)[2] for g in range(group)]
    own_rows = spread[pl.ds(pl.multiple_of(z * group * w, w), group * w), :]
    own_one, own_two = own_rows[:, 0:w], own_rows[:, w:2 * w]
    summed_one = jnp.concatenate([s[:, 0:w] for s in sums], axis=0)
    for g in range(group):
        ag[m, g] = (sums[g][:, 0:w] * -hits_one[g]).astype(bf16)
    part_one = (gram_one + dot_t(own_one, summed_one.astype(bf16))).astype(bf16)
    ag[m, group] = part_one
    z_one[...] = part_one

    def ag_copy(t):
        return pltpu.make_async_remote_copy(
            src_ref=ag.at[m], dst_ref=ag.at[m], send_sem=ag_s.at[t], recv_sem=ag_r.at[m],
            device_id=peer(t)[1], device_id_type=MESH,
        )

    each(members, lambda t: ag_copy(t).start(), 1)

    def z_copy(source, target, sem, recv):
        return pltpu.make_async_remote_copy(
            src_ref=source, dst_ref=target.at[z], send_sem=z_s.at[sem], recv_sem=recv.at[z],
            device_id=(home * group + x, c), device_id_type=MESH,
        )

    first = z_copy(z_one, zr_one, 0, zr_one_r)
    second = z_copy(z_two, zr_two, 1, zr_two_r)

    @pl.when(jnp.logical_not(mine))
    def _():
        first.start()

    def ag_wait(t):
        q, _ = peer(t)
        pltpu.make_async_copy(ag.at[q], ag.at[q], ag_r.at[q]).wait()

    each(members, ag_wait, 1)

    slot = jnp.int32(0)
    for row in range(tops):
        slot = jnp.where(up == row, place(row), slot)
    inherited = jnp.concatenate([ag[slot, g] for g in range(group)], axis=0)
    up_diag = ag[slot, group]
    summed_two = jnp.concatenate([s[:, w:2 * w] for s in sums], axis=0) + dot(
        inherited, scaled_parent
    )
    carried = dot_t(inherited, own_two) + dot(up_diag, scaled_parent)
    part_two = (
        gram_two
        + dot_t(own_two, summed_two.astype(bf16))
        + dot_t(scaled_parent, carried.astype(bf16))
    )
    z_two[0] = carried.astype(bf16)
    z_two[1] = part_two.astype(bf16)

    @pl.when(jnp.logical_not(mine))
    def _():
        second.start()

    for g in range(group):
        two_send[g] = (summed_two[g * w:(g + 1) * w] * -hits_two[g]).astype(bf16)
    two_recv[m] = two_send[x]

    def two_copy(t):
        q, device = peer(t)
        return pltpu.make_async_remote_copy(
            src_ref=two_send.at[q // pcols], dst_ref=two_recv.at[m], send_sem=two_s.at[t],
            recv_sem=two_r.at[m], device_id=device, device_id_type=MESH,
        )

    each(members, lambda t: two_copy(t).start(), 1)

    def fin_copy(t):
        return pltpu.make_async_remote_copy(
            src_ref=fin, dst_ref=fin, send_sem=fin_s.at[t], recv_sem=fin_r,
            device_id=(p, (c + t) % pcols), device_id_type=MESH,
        )

    @pl.when(mine)
    def _():
        def gather_wait(ref, sem):
            def step(t):
                other = (z + t) % planes
                pltpu.make_async_copy(ref.at[other], ref.at[other], sem.at[other]).wait()
            each(planes, step, 1)

        gather_wait(zr_one, zr_one_r)
        zr_one[z] = z_one[...]
        fin[0] = jnp.sum(zr_one[...].astype(f32), axis=0).astype(bf16)
        gather_wait(zr_two, zr_two_r)
        zr_two[z] = z_two[...]
        fin[1:3] = jnp.sum(zr_two[...].astype(f32), axis=0).astype(bf16)
        each(pcols, lambda t: fin_copy(t).start(), 1)

    def out_one(row):
        top_one[0, row] = ag[place(row), x]

    each(tops, out_one)

    def two_wait(t):
        q, _ = peer(t)
        pltpu.make_async_copy(two_recv.at[q], two_recv.at[q], two_r.at[q]).wait()

    each(members, two_wait, 1)

    def out_two(row):
        top_two[0, row] = two_recv[place(row)]

    each(tops, out_two)

    @pl.when(jnp.logical_not(mine))
    def _():
        pltpu.make_async_copy(fin, fin, fin_r).wait()

    diag_one[0] = fin[0].astype(f32)
    parent_out[0] = -fin[1].astype(f32)
    diag_two[0] = fin[2].astype(f32)

    for copy_to in (msg_copy, par_copy):
        each(planes, lambda t: copy_to(planes - t).wait_send(), 1)

    @pl.when(jnp.logical_not(stays))
    def _():
        msg_copy(0).wait_send()
        par_copy(0).wait_send()

    def drain(t):
        sig_copy(t).wait_send()
        ag_copy(t).wait_send()
        two_copy(t).wait_send()

    each(members, drain, 1)

    @pl.when(jnp.logical_not(mine))
    def _():
        first.wait_send()
        second.wait_send()

    @pl.when(mine)
    def _():
        each(pcols, lambda t: fin_copy(t).wait_send(), 1)


def body(
    prows, pcols,
    sigma_top, factor_one, inverse_one, pattern_one, factor_two, parent_block, inverse_two,
    parent_two, keep_two,
):
    w = sigma_top.shape[2]
    total_one = pattern_one.shape[0]
    tops = prows * sigma_top.shape[0]
    group = total_one // pcols
    planes = prows // group
    members = group * pcols
    tiles = factor_one.shape[1]
    assert sigma_top.shape[0] == factor_one.shape[0] == factor_two.shape[0] == 1
    assert planes == pcols and members == tops == total_one == parent_two.shape[0]
    vmem = pl.BlockSpec(memory_space=pltpu.VMEM)
    smem = pl.BlockSpec(memory_space=pltpu.SMEM)
    dma = pltpu.SemaphoreType.DMA
    return pl.pallas_call(
        functools.partial(kernel, prows, pcols, group),
        out_shape=(
            jax.ShapeDtypeStruct((1, total_one, w, w), bf16),
            jax.ShapeDtypeStruct((1, w, w), f32),
            jax.ShapeDtypeStruct((1, total_one, w, w), bf16),
            jax.ShapeDtypeStruct((1, w, w), f32),
            jax.ShapeDtypeStruct((1, w, w), f32),
        ),
        in_specs=[vmem] * 6 + [smem] * 3,
        out_specs=(vmem,) * 5,
        scratch_shapes=[
            pltpu.VMEM((2 * tiles, w, w), bf16),
            pltpu.VMEM((w // pcols, w), bf16),
            pltpu.VMEM((pcols, 2 * tiles, w, w), bf16),
            pltpu.VMEM((pcols, w // pcols, w), bf16),
            pltpu.VMEM((group, tops, w, w), bf16),
            pltpu.VMEM((tops * w, 2 * w), bf16),
            pltpu.VMEM((group, w, 2 * w), f32),
            pltpu.VMEM((members, group + 1, w, w), bf16),
            pltpu.VMEM((group, w, w), bf16),
            pltpu.VMEM((members, w, w), bf16),
            pltpu.VMEM((w, w), bf16),
            pltpu.VMEM((2, w, w), bf16),
            pltpu.VMEM((planes, w, w), bf16),
            pltpu.VMEM((planes, 2, w, w), bf16),
            pltpu.VMEM((3, w, w), bf16),
            dma((planes,)), dma((planes,)), dma((pcols,)), dma((pcols,)),
            dma((members,)), dma((members,)),
            dma((members,)), dma((members,)),
            dma((members,)), dma((members,)),
            dma((2,)), dma((planes,)), dma((planes,)),
            dma((pcols,)), dma,
        ],
        compiler_params=pltpu.CompilerParams(
            collective_id=0, has_side_effects=True, vmem_limit_bytes=40 * 1024 * 1024
        ),
    )(
        sigma_top, factor_one, inverse_one, factor_two, parent_block, inverse_two,
        pattern_one, parent_two, keep_two,
    )


def solution(mesh):
    in_specs = (
        P("prow", "pcol", None, None),
        P("prow", "pcol", None, None),
        P("prow", None, None),
        P(),
        P("prow", "pcol", None, None),
        P("prow", None, None),
        P("prow", None, None),
        P(),
        P(),
    )
    out_specs = (
        P("prow", None, None, None),
        P("prow", None, None),
        P("prow", None, None, None),
        P("prow", None, None),
        P("prow", None, None),
    )
    step = functools.partial(body, mesh.shape["prow"], mesh.shape["pcol"])
    return jax.shard_map(step, mesh=mesh, in_specs=in_specs, out_specs=out_specs, check_vma=False)
```

time: 454 us -> 48.8 us (0.11)
  waiting for transfers between devices: 313 us -> 0 us
  blocking collectives: 103 us -> 0 us
  Pallas kernels: 0 us -> 37.5 us
  between operations: 14.4 us -> 0.66 us
  matrix products: 13.2 us -> 0 us
    psum x4 -> x0, waiting for transfers between devices: 187 us -> none  [the longest x1 129 us: body(): diagonal_all = lax.psum(partial_diag, ('prow', 'pcol'))]
    reduce_scatter x2 -> x0, waiting for transfers between devices: 126 us -> none  [the longest x1 63.8 us: body(): lax.psum_scatter(quadratic_two.astype(jnp.bfloat16), 'prow', scatter_dime...]
    all_gather x5 -> x0, blocking collectives: 103 us -> none  [the longest x1 31.9 us: body(): spread_all = lax.all_gather(spread_one, 'prow', axis=0, tiled=True)]
    pallas_call x0 -> x1, Pallas kernels: none -> 37.5 us  [body(): pl.pallas_call(functools.partial(kernel, prows, pcols, group), out_shape=...]
    dot_general x19 -> x0, matrix products: 13.2 us -> none  [the longest x1 1.85 us: body(): jnp.einsum('ij,jwv->iwv', own_hot, diagonal_all, precision=highest)]
    unnamed x26 -> x23, local copies, waits for them, and re-layouts: 5.32 us -> 10.1 us
  transfers between devices with their start and end apart: 6 -> 0, of which waited for: 5 -> 0; matrix products, arithmetic and copies ran while one was open for 3% -> 0% of each run, Pallas kernels for 0% -> 0%
where the time goes in v1:
time: 48.8 us; the launch traced here: 48.2 us
  Pallas kernels  37.5 us (77%)
  local copies, waits for them, and re-layouts  10.1 us (21%)
  between operations  0.66 us (1%)
    pallas_call x1, Pallas kernels, body(): pl.pallas_call(functools.partial(kernel, prows, pcols, group), out_shape=...  37.5 us
    unnamed x23, local copies, waits for them, and re-layouts  10.1 us

profile of v1, /device:TPU:0, one launch (start us, length us, event | category | flops | bytes accessed | tf_op | source)
XLA Modules:
  0.0 48.2 jit_solution(11071662433224709720)
XLA Ops:
  0.6 0.0 copy-start
  0.6 0.8 %copy-done = bf16[1,2,128,128]{3,2,1,0:T(8,128)(2,1)S(1)} copy-done((bf16[1,2,128,128]{3,2,1,0:T(8,128)(2,1)S(1)}, bf16[1,2,128,128]{3,2,1,0:T(8,128)(2,1)}, u32[]{:S(2)}) %copy-start) | copy-done | bytes 65560
  1.5 0.0 copy-start.1
  1.5 0.8 %copy-done.1 = bf16[1,2,128,128]{3,2,1,0:T(8,128)(2,1)S(1)} copy-done((bf16[1,2,128,128]{3,2,1,0:T(8,128)(2,1)S(1)}, bf16[1,2,128,128]{3,2,1,0:T(8,128)(2,1)}, u32[]{:S(2)}) %copy-start.1) | copy-done | bytes 65560
  2.3 0.0 copy-start.2
  2.3 0.8 %copy-done.2 = bf16[1,2,128,128]{3,2,1,0:T(8,128)(2,1)S(1)} copy-done((bf16[1,2,128,128]{3,2,1,0:T(8,128)(2,1)S(1)}, bf16[1,2,128,128]{3,2,1,0:T(8,128)(2,1)}, u32[]{:S(2)}) %copy-start.2) | copy-done | bytes 65560
  3.2 0.0 copy-start.3
  3.2 0.8 %copy-done.3 = bf16[1,128,128]{2,1,0:T(8,128)(2,1)S(1)} copy-done((bf16[1,128,128]{2,1,0:T(8,128)(2,1)S(1)}, bf16[1,128,128]{2,1,0:T(8,128)(2,1)}, u32[]{:S(2)}) %copy-start.3) | copy-done | bytes 32792
  3.9 0.0 copy-start.4
  3.9 0.8 %copy-done.4 = bf16[1,128,128]{2,1,0:T(8,128)(2,1)S(1)} copy-done((bf16[1,128,128]{2,1,0:T(8,128)(2,1)S(1)}, bf16[1,128,128]{2,1,0:T(8,128)(2,1)}, u32[]{:S(2)}) %copy-start.4) | copy-done | bytes 32792
  4.7 0.0 copy-start.5
  4.7 0.8 %copy-done.5 = bf16[1,128,128]{2,1,0:T(8,128)(2,1)S(1)} copy-done((bf16[1,128,128]{2,1,0:T(8,128)(2,1)S(1)}, bf16[1,128,128]{2,1,0:T(8,128)(2,1)}, u32[]{:S(2)}) %copy-start.5) | copy-done | bytes 32792
  5.4 0.0 copy-start.6
  5.4 0.7 %copy-done.6 = s32[8,8]{1,0:T(8,128)S(1)} copy-done((s32[8,8]{1,0:T(8,128)S(1)}, s32[8,8]{1,0:T(8,128)}, u32[]{:S(2)}) %copy-start.6) | copy-done | bytes 280
  6.1 0.0 copy-start.7
  6.1 0.7 %copy-done.7 = s32[8,8]{1,0:T(8,128)S(1)} copy-done((s32[8,8]{1,0:T(8,128)S(1)}, s32[8,8]{1,0:T(8,128)}, u32[]{:S(2)}) %copy-start.7) | copy-done | bytes 280
  6.8 0.0 copy-start.8
  6.8 0.7 %copy-done.8 = s32[8]{0:T(128)S(1)} copy-done((s32[8]{0:T(128)S(1)}, s32[8]{0:T(128)}, u32[]{:S(2)}) %copy-start.8) | copy-done | bytes 56
  7.5 37.5 %shard_map.128 = (bf16[1,8,128,128]{3,2,1,0:T(8,128)(2,1)S(1)}, f32[1,128,128]{2,1,0:T(8,128)S(1)}, bf16[1,8,128,128]{3,2,1,0:T(8,128)(2,1)S(1)}, f32[1,128,128]{2,1,0:T(8,128)S(1)}, f32[1,128,128]{2,1,0:T(8,128)S(1)}) custom-call(bf16[1,2,128,128]{3,2,1,0:T(8,128)(2,1)S(1)} %copy-done, bf16[1,2,128,128]{3,2,1,0:T(8,128)(2,1)S(1)} %copy-done.1, ...), custom_call_target="tpu_custom_call" | custom-call | tf_op jit(solution)/shard_map/pallas_call | solution.py:358
  44.9 0.7 %copy.19 = bf16[1,8,128,128]{3,2,1,0:T(8,128)(2,1)} copy(bf16[1,8,128,128]{3,2,1,0:T(8,128)(2,1)S(1)} %get-tuple-element.10) | data formatting | bytes 524288
  45.6 0.6 %copy.20 = f32[1,128,128]{2,1,0:T(8,128)} copy(f32[1,128,128]{2,1,0:T(8,128)S(1)} %get-tuple-element.11) | data formatting | bytes 131072
  46.3 0.7 %copy.21 = bf16[1,8,128,128]{3,2,1,0:T(8,128)(2,1)} copy(bf16[1,8,128,128]{3,2,1,0:T(8,128)(2,1)S(1)} %get-tuple-element.12) | data formatting | bytes 524288
  47.0 0.6 %copy.22 = f32[1,128,128]{2,1,0:T(8,128)} copy(f32[1,128,128]{2,1,0:T(8,128)S(1)} %get-tuple-element.13) | data formatting | bytes 131072
  47.6 0.6 %copy.23 = f32[1,128,128]{2,1,0:T(8,128)} copy(f32[1,128,128]{2,1,0:T(8,128)S(1)} %get-tuple-element.14) | data formatting | bytes 131072
Async XLA Ops:
  0.6 0.8 %copy-start = (bf16[1,2,128,128]{3,2,1,0:T(8,128)(2,1)S(1)}, bf16[1,2,128,128]{3,2,1,0:T(8,128)(2,1)}, u32[]{:S(2)}) copy-start(bf16[1,2,128,128]{3,2,1,0:T(8,128)(2,1)} %sigma.1) | copy-start | bytes 196612
  1.5 0.8 %copy-start.1 = (bf16[1,2,128,128]{3,2,1,0:T(8,128)(2,1)S(1)}, bf16[1,2,128,128]{3,2,1,0:T(8,128)(2,1)}, u32[]{:S(2)}) copy-start(bf16[1,2,128,128]{3,2,1,0:T(8,128)(2,1)} %factor_one.1) | copy-start | bytes 196612
  2.3 0.8 %copy-start.2 = (bf16[1,2,128,128]{3,2,1,0:T(8,128)(2,1)S(1)}, bf16[1,2,128,128]{3,2,1,0:T(8,128)(2,1)}, u32[]{:S(2)}) copy-start(bf16[1,2,128,128]{3,2,1,0:T(8,128)(2,1)} %factor_two.1) | copy-start | bytes 196612
  3.2 0.8 %copy-start.3 = (bf16[1,128,128]{2,1,0:T(8,128)(2,1)S(1)}, bf16[1,128,128]{2,1,0:T(8,128)(2,1)}, u32[]{:S(2)}) copy-start(bf16[1,128,128]{2,1,0:T(8,128)(2,1)} %inverse_one.1) | copy-start | bytes 98308
  3.9 0.8 %copy-start.4 = (bf16[1,128,128]{2,1,0:T(8,128)(2,1)S(1)}, bf16[1,128,128]{2,1,0:T(8,128)(2,1)}, u32[]{:S(2)}) copy-start(bf16[1,128,128]{2,1,0:T(8,128)(2,1)} %parent_block.1) | copy-start | bytes 98308
  4.7 0.8 %copy-start.5 = (bf16[1,128,128]{2,1,0:T(8,128)(2,1)S(1)}, bf16[1,128,128]{2,1,0:T(8,128)(2,1)}, u32[]{:S(2)}) copy-start(bf16[1,128,128]{2,1,0:T(8,128)(2,1)} %inverse_two.1) | copy-start | bytes 98308
  5.4 0.7 %copy-start.6 = (s32[8,8]{1,0:T(8,128)S(1)}, s32[8,8]{1,0:T(8,128)}, u32[]{:S(2)}) copy-start(s32[8,8]{1,0:T(8,128)} %pattern.1) | copy-start | bytes 772
  6.1 0.7 %copy-start.7 = (s32[8,8]{1,0:T(8,128)S(1)}, s32[8,8]{1,0:T(8,128)}, u32[]{:S(2)}) copy-start(s32[8,8]{1,0:T(8,128)} %keep.1) | copy-start | bytes 772
  6.8 0.7 %copy-start.8 = (s32[8]{0:T(128)S(1)}, s32[8]{0:T(128)}, u32[]{:S(2)}) copy-start(s32[8]{0:T(128)} %parent.1) | copy-start | bytes 100

commit v2 on v1

--- a/solution.py
+++ b/solution.py
@@ -30,17 +30,18 @@
 
 def kernel(
     prows, pcols, group,
-    sigma, factor_one, inverse_one, factor_two, parent_block, inverse_two,
-    pattern, parent, keep,
+    sigma, factor_one_in, inverse_one_in, factor_two_in, parent_block_in, inverse_two_in,
+    pattern_in, parent_in, keep_in,
     top_one, diag_one, top_two, parent_out, diag_two,
-    msg, par_msg, rx, par_rx, sig, spread, total, ag, two_send, two_recv, z_one, z_two, zr_one, zr_two, fin,
+    factor_one, inverse_one, factor_two, parent_block, inverse_two, pattern, parent, keep,
+    load_s, store_s, blocks, msg, par_msg, rx, par_rx, sig, spread, total, ag, two_send, two_recv, z_one, z_two, zr_one, zr_two, fin,
     msg_s, par_s, msg_r, par_r, sig_s, sig_r, ag_s, ag_r, two_s, two_r, z_s, zr_one_r, zr_two_r, fin_s, fin_r,
 ):
     planes = prows // group
     half = pcols // 2
     cols = sigma.shape[1]
     w = sigma.shape[2]
-    tiles = factor_one.shape[1]
+    tiles = factor_one_in.shape[1]
     reach = pattern.shape[1]
     tops = prows
     members = group * pcols
@@ -63,6 +64,19 @@
         q = (m + t) % members
         return q, (z * group + q // pcols, q % pcols)
 
+    own_cols = pl.ds(c * cols, cols)
+    loads = [
+        pltpu.make_async_copy(source, target, load_s.at[n])
+        for n, (source, target) in enumerate([
+            (inverse_two_in, inverse_two), (factor_two_in, factor_two),
+            (inverse_one_in, inverse_one), (factor_one_in, factor_one),
+            (parent_block_in, parent_block), (sigma.at[0], sig.at[x, own_cols]),
+            (pattern_in, pattern), (parent_in, parent), (keep_in, keep),
+        ])
+    ]
+    for load in loads:
+        load.start()
+
     barrier = pltpu.get_barrier_semaphore()
 
     def greet_plane(t):
@@ -76,6 +90,9 @@
 
     each((planes - 1) * pcols, greet_line)
     each(members, greet_plane, 1)
+
+    for load in loads:
+        load.wait()
 
     keep_lower = lax.broadcasted_iota(jnp.int32, (w, w), 0) >= lax.broadcasted_iota(
         jnp.int32, (w, w), 1
@@ -87,8 +104,6 @@
         msg[tiles + k] = dot(factor_two[0, k], lower_two).astype(bf16)
     part = parent_block[0, pl.ds(pl.multiple_of(c * slice_rows, slice_rows), slice_rows), :]
     par_msg[...] = dot(part, lower_two).astype(bf16)
-    own_cols = pl.ds(c * cols, cols)
-    sig[x, own_cols] = sigma[0]
 
     pl.semaphore_wait(barrier, (planes - 1) * pcols + members - 1)
 
@@ -233,6 +248,11 @@
 
     each(members, ag_wait, 1)
 
+    def out_one(row):
+        return pltpu.make_async_copy(ag.at[place(row), x], top_one.at[0, row], store_s.at[row])
+
+    each(tops, lambda row: out_one(row).start())
+
     slot = jnp.int32(0)
     for row in range(tops):
         slot = jnp.where(up == row, place(row), slot)
@@ -289,10 +309,6 @@
         fin[1:3] = jnp.sum(zr_two[...].astype(f32), axis=0).astype(bf16)
         each(pcols, lambda t: fin_copy(t).start(), 1)
 
-    def out_one(row):
-        top_one[0, row] = ag[place(row), x]
-
-    each(tops, out_one)
 
     def two_wait(t):
         q, _ = peer(t)
@@ -301,18 +317,30 @@
     each(members, two_wait, 1)
 
     def out_two(row):
-        top_two[0, row] = two_recv[place(row)]
-
-    each(tops, out_two)
+        return pltpu.make_async_copy(
+            two_recv.at[place(row)], top_two.at[0, row], store_s.at[tops + row]
+        )
+
+    each(tops, lambda row: out_two(row).start())
 
     @pl.when(jnp.logical_not(mine))
     def _():
         pltpu.make_async_copy(fin, fin, fin_r).wait()
 
-    diag_one[0] = fin[0].astype(f32)
-    parent_out[0] = -fin[1].astype(f32)
-    diag_two[0] = fin[2].astype(f32)
-
+    blocks[0] = fin[0].astype(f32)
+    blocks[1] = -fin[1].astype(f32)
+    blocks[2] = fin[2].astype(f32)
+    block_copies = [
+        pltpu.make_async_copy(blocks.at[n], ref.at[0], store_s.at[2 * tops + n])
+        for n, ref in enumerate((diag_one, parent_out, diag_two))
+    ]
+    for copy in block_copies:
+        copy.start()
+
+    each(tops, lambda row: out_one(row).wait())
+    each(tops, lambda row: out_two(row).wait())
+    for copy in block_copies:
+        copy.wait()
     for copy_to in (msg_copy, par_copy):
         each(planes, lambda t: copy_to(planes - t).wait_send(), 1)
 
@@ -336,6 +364,14 @@
     @pl.when(mine)
     def _():
         each(pcols, lambda t: fin_copy(t).wait_send(), 1)
+
+
+def write_out(*refs):
+    copies = [pltpu.make_async_copy(refs[n], refs[5 + n], refs[10].at[n]) for n in range(5)]
+    for copy in copies:
+        copy.start()
+    for copy in copies:
+        copy.wait()
 
 
 def body(
@@ -352,21 +388,32 @@
     tiles = factor_one.shape[1]
     assert sigma_top.shape[0] == factor_one.shape[0] == factor_two.shape[0] == 1
     assert planes == pcols and members == tops == total_one == parent_two.shape[0]
-    vmem = pl.BlockSpec(memory_space=pltpu.VMEM)
-    smem = pl.BlockSpec(memory_space=pltpu.SMEM)
+    hbm = pl.BlockSpec(memory_space=pltpu.HBM)
+    shapes = (
+        jax.ShapeDtypeStruct((1, total_one, w, w), bf16),
+        jax.ShapeDtypeStruct((1, w, w), f32),
+        jax.ShapeDtypeStruct((1, total_one, w, w), bf16),
+        jax.ShapeDtypeStruct((1, w, w), f32),
+        jax.ShapeDtypeStruct((1, w, w), f32),
+    )
     dma = pltpu.SemaphoreType.DMA
-    return pl.pallas_call(
+    results = pl.pallas_call(
         functools.partial(kernel, prows, pcols, group),
-        out_shape=(
-            jax.ShapeDtypeStruct((1, total_one, w, w), bf16),
-            jax.ShapeDtypeStruct((1, w, w), f32),
-            jax.ShapeDtypeStruct((1, total_one, w, w), bf16),
-            jax.ShapeDtypeStruct((1, w, w), f32),
-            jax.ShapeDtypeStruct((1, w, w), f32),
-        ),
-        in_specs=[vmem] * 6 + [smem] * 3,
-        out_specs=(vmem,) * 5,
+        out_shape=shapes,
+        in_specs=[hbm] * 9,
+        out_specs=(hbm,) * 5,
         scratch_shapes=[
+            pltpu.VMEM(factor_one.shape, bf16),
+            pltpu.VMEM(inverse_one.shape, bf16),
+            pltpu.VMEM(factor_two.shape, bf16),
+            pltpu.VMEM(parent_block.shape, bf16),
+            pltpu.VMEM(inverse_two.shape, bf16),
+            pltpu.SMEM(pattern_one.shape, jnp.int32),
+            pltpu.SMEM(parent_two.shape, jnp.int32),
+            pltpu.SMEM(keep_two.shape, jnp.int32),
+            dma((9,)),
+            dma((2 * total_one + 3,)),
+            pltpu.VMEM((3, w, w), f32),
             pltpu.VMEM((2 * tiles, w, w), bf16),
             pltpu.VMEM((w // pcols, w), bf16),
             pltpu.VMEM((pcols, 2 * tiles, w, w), bf16),
@@ -390,12 +437,19 @@
             dma((pcols,)), dma,
         ],
         compiler_params=pltpu.CompilerParams(
-            collective_id=0, has_side_effects=True, vmem_limit_bytes=40 * 1024 * 1024
+            collective_id=0, has_side_effects=True
         ),
     )(
         sigma_top, factor_one, inverse_one, factor_two, parent_block, inverse_two,
         pattern_one, parent_two, keep_two,
     )
+    return pl.pallas_call(
+        write_out,
+        out_shape=shapes,
+        in_specs=[hbm] * 5,
+        out_specs=(hbm,) * 5,
+        scratch_shapes=[dma((5,))],
+    )(*results)
 
 
 def solution(mesh):

time: 48.8 us -> 61.4 us (1.26)
  Pallas kernels: 37.5 us -> 60.1 us
  local copies, waits for them, and re-layouts: 10.1 us -> 0 us
    pallas_call x0 -> x1, Pallas kernels: none -> 23 us  [body(): pl.pallas_call(write_out, out_shape=shapes, in_specs=[hbm] * 5, out_specs...]
    unnamed x23 -> x0, local copies, waits for them, and re-layouts: 10.1 us -> none
where the time goes in v2:
time: 61.4 us; the launch traced here: 60.7 us
  Pallas kernels  60.1 us (98%)
  between operations  0.64 us (1%)
    pallas_call x1, Pallas kernels, body(): pl.pallas_call(functools.partial(kernel, prows, pcols, group), out_shape=...  37.1 us
    pallas_call x1, Pallas kernels, body(): pl.pallas_call(write_out, out_shape=shapes, in_specs=[hbm] * 5, out_specs...  23 us

profile of v2, /device:TPU:0, one launch (start us, length us, event | category | flops | bytes accessed | tf_op | source)
XLA Modules:
  0.0 60.7 jit_solution(13595232118953129206)
XLA Ops:
  0.6 37.1 %shard_map.128 = (bf16[1,8,128,128]{3,2,1,0:T(8,128)(2,1)}, f32[1,128,128]{2,1,0:T(8,128)}, bf16[1,8,128,128]{3,2,1,0:T(8,128)(2,1)}, f32[1,128,128]{2,1,0:T(8,128)}, f32[1,128,128]{2,1,0:T(8,128)}) custom-call(bf16[1,2,128,128]{3,2,1,0:T(8,128)(2,1)} %sigma.1, bf16[1,2,128,128]{3,2,1,0:T(8,128)(2,1)} %factor_one_in.1, bf16[1,128,128]{2,1,0:T(8,128)(2,1)} %inverse_one_in.1, ...), custom_call_target="tpu_custom_call" | custom-call | tf_op jit(solution)/shard_map/pallas_call | solution.py:400
  37.7 23.0 %shard_map.129 = (bf16[1,8,128,128]{3,2,1,0:T(8,128)(2,1)}, f32[1,128,128]{2,1,0:T(8,128)}, bf16[1,8,128,128]{3,2,1,0:T(8,128)(2,1)}, f32[1,128,128]{2,1,0:T(8,128)}, f32[1,128,128]{2,1,0:T(8,128)}) custom-call(bf16[1,8,128,128]{3,2,1,0:T(8,128)(2,1)} %get-tuple-element.10.refs_0_, f32[1,128,128]{2,1,0:T(8,128)} %get-tuple-element.11.refs_1_, ...), custom_call_target="tpu_custom_call" | custom-call | tf_op jit(solution)/shard_map/pallas_call | solution.py:446

commit v3 on v2

--- a/solution.py
+++ b/solution.py
@@ -367,11 +367,16 @@
 
 
 def write_out(*refs):
-    copies = [pltpu.make_async_copy(refs[n], refs[5 + n], refs[10].at[n]) for n in range(5)]
-    for copy in copies:
-        copy.start()
-    for copy in copies:
-        copy.wait()
+    sources, targets, held = refs[0:5], refs[5:10], refs[10:15]
+    loads = [pltpu.make_async_copy(sources[n], held[n], refs[15].at[n]) for n in range(5)]
+    stores = [pltpu.make_async_copy(held[n], targets[n], refs[16].at[n]) for n in range(5)]
+    for load in loads:
+        load.start()
+    for load, store in zip(loads, stores):
+        load.wait()
+        store.start()
+    for store in stores:
+        store.wait()
 
 
 def body(
@@ -448,7 +453,7 @@
         out_shape=shapes,
         in_specs=[hbm] * 5,
         out_specs=(hbm,) * 5,
-        scratch_shapes=[dma((5,))],
+        scratch_shapes=[pltpu.VMEM(s.shape, s.dtype) for s in shapes] + [dma((5,)), dma((5,))],
     )(*results)
 
 

time: 61.4 us -> 40.3 us (0.66)
  Pallas kernels: 60.1 us -> 38.9 us
    pallas_call x1, Pallas kernels: 23 us -> 1.89 us  [body(): pl.pallas_call(write_out, out_shape=shapes, in_specs=[hbm] * 5, out_specs...]
where the time goes in v3:
time: 40.3 us; the launch traced here: 39.6 us
  Pallas kernels  38.9 us (97%)
  between operations  0.64 us (2%)
    pallas_call x1, Pallas kernels, body(): pl.pallas_call(functools.partial(kernel, prows, pcols, group), out_shape=...  37.1 us
    pallas_call x1, Pallas kernels, body(): pl.pallas_call(write_out, out_shape=shapes, in_specs=[hbm] * 5, out_specs...  1.89 us

profile of v3, /device:TPU:0, one launch (start us, length us, event | category | flops | bytes accessed | tf_op | source)
XLA Modules:
  0.0 39.6 jit_solution(4465292607033015840)
XLA Ops:
  0.6 37.1 %shard_map.128 = (bf16[1,8,128,128]{3,2,1,0:T(8,128)(2,1)}, f32[1,128,128]{2,1,0:T(8,128)}, bf16[1,8,128,128]{3,2,1,0:T(8,128)(2,1)}, f32[1,128,128]{2,1,0:T(8,128)}, f32[1,128,128]{2,1,0:T(8,128)}) custom-call(bf16[1,2,128,128]{3,2,1,0:T(8,128)(2,1)} %sigma.1, bf16[1,2,128,128]{3,2,1,0:T(8,128)(2,1)} %factor_one_in.1, bf16[1,128,128]{2,1,0:T(8,128)(2,1)} %inverse_one_in.1, ...), custom_call_target="tpu_custom_call" | custom-call | tf_op jit(solution)/shard_map/pallas_call | solution.py:405
  37.7 1.9 %shard_map.129 = (bf16[1,8,128,128]{3,2,1,0:T(8,128)(2,1)}, f32[1,128,128]{2,1,0:T(8,128)}, bf16[1,8,128,128]{3,2,1,0:T(8,128)(2,1)}, f32[1,128,128]{2,1,0:T(8,128)}, f32[1,128,128]{2,1,0:T(8,128)}) custom-call(bf16[1,8,128,128]{3,2,1,0:T(8,128)(2,1)} %get-tuple-element.10.refs_0_, f32[1,128,128]{2,1,0:T(8,128)} %get-tuple-element.11.refs_1_, ...), custom_call_target="tpu_custom_call" | custom-call | tf_op jit(solution)/shard_map/pallas_call | solution.py:451

commit v4 on v3

--- a/solution.py
+++ b/solution.py
@@ -34,8 +34,8 @@
     pattern_in, parent_in, keep_in,
     top_one, diag_one, top_two, parent_out, diag_two,
     factor_one, inverse_one, factor_two, parent_block, inverse_two, pattern, parent, keep,
-    load_s, store_s, blocks, msg, par_msg, rx, par_rx, sig, spread, total, ag, two_send, two_recv, z_one, z_two, zr_one, zr_two, fin,
-    msg_s, par_s, msg_r, par_r, sig_s, sig_r, ag_s, ag_r, two_s, two_r, z_s, zr_one_r, zr_two_r, fin_s, fin_r,
+    load_s, store_s, blocks, msg, par_msg, rx, rx_two, par_rx, sig, spread_one, spread_two, total, ag, two_send, two_recv, z_one, z_two, zr_one, zr_two, fin,
+    msg_s, msg_two_s, par_s, msg_r, msg_two_r, par_r, sig_s, sig_r, ag_s, ag_r, two_s, two_r, z_s, zr_one_r, zr_two_r, fin_s, fin_r,
 ):
     planes = prows // group
     half = pcols // 2
@@ -77,6 +77,37 @@
     for load in loads:
         load.start()
 
+    chips = members // 2
+    other_core = (z * group + x, c + 1 - 2 * (c % 2))
+
+    def far(t):
+        q = (m + 2 * t) % members
+        return q, (z * group + q // pcols, q % pcols)
+
+    def near(t):
+        return (2 * (m // 2) + 1 - m % 2 + 2 * t) % members
+
+    def plane_start(copy):
+        each(chips, lambda t: copy(t, far(t)[1]).start(), 1)
+        copy(0, other_core).start()
+
+    def plane_wait(wait, forward):
+        def pass_on(t):
+            q, _ = far(t)
+            wait(q)
+            forward(t, q).start()
+
+        each(chips, pass_on, 1)
+        each(chips, lambda t: wait(near(t)))
+
+    def plane_drain(copy, forward):
+        def drain(t):
+            copy(t, far(t)[1]).wait_send()
+            forward(t, far(t)[0]).wait_send()
+
+        each(chips, drain, 1)
+        copy(0, other_core).wait_send()
+
     barrier = pltpu.get_barrier_semaphore()
 
     def greet_plane(t):
@@ -110,7 +141,16 @@
     def msg_copy(t):
         other = (z + t) % planes
         return pltpu.make_async_remote_copy(
-            src_ref=msg, dst_ref=rx.at[c], send_sem=msg_s.at[t], recv_sem=msg_r.at[c],
+            src_ref=msg.at[0:tiles], dst_ref=rx.at[c], send_sem=msg_s.at[t],
+            recv_sem=msg_r.at[c],
+            device_id=(other * group + x, target_col), device_id_type=MESH,
+        )
+
+    def msg_two_copy(t):
+        other = (z + t) % planes
+        return pltpu.make_async_remote_copy(
+            src_ref=msg.at[tiles:2 * tiles], dst_ref=rx_two.at[c],
+            send_sem=msg_two_s.at[t], recv_sem=msg_two_r.at[c],
             device_id=(other * group + x, target_col), device_id_type=MESH,
         )
 
@@ -122,26 +162,39 @@
         )
 
     stays = target_col == c
-    for copy_to in (msg_copy, par_copy):
-        each(planes, lambda t: copy_to(planes - t).start(), 1)
-
-    @pl.when(jnp.logical_not(stays))
-    def _():
-        msg_copy(0).start()
-        par_copy(0).start()
-
-    @pl.when(stays)
-    def _():
-        pltpu.make_async_copy(msg, rx.at[c], msg_r.at[c]).start()
-        pltpu.make_async_copy(par_msg, par_rx.at[c], par_r.at[c]).start()
-
-    def sig_copy(t):
-        return pltpu.make_async_remote_copy(
-            src_ref=sigma.at[0], dst_ref=sig.at[x, own_cols], send_sem=sig_s.at[t],
-            recv_sem=sig_r.at[m], device_id=peer(t)[1], device_id_type=MESH,
-        )
-
-    each(members, lambda t: sig_copy(t).start(), 1)
+
+    def send_tiles(copies, local):
+        for copy_to in copies:
+            each(planes, lambda t: copy_to(planes - t).start(), 1)
+
+        @pl.when(jnp.logical_not(stays))
+        def _():
+            for copy_to in copies:
+                copy_to(0).start()
+
+        @pl.when(stays)
+        def _():
+            for source, target, sem in local:
+                pltpu.make_async_copy(source, target, sem).start()
+
+    send_tiles([msg_copy], [(msg.at[0:tiles], rx.at[c], msg_r.at[c])])
+
+    def sig_slot(q):
+        return sig.at[q // pcols, pl.ds((q % pcols) * cols, cols)]
+
+    def sig_copy(t, device):
+        return pltpu.make_async_remote_copy(
+            src_ref=sigma.at[0], dst_ref=sig_slot(m), send_sem=sig_s.at[t],
+            recv_sem=sig_r.at[m], device_id=device, device_id_type=MESH,
+        )
+
+    def sig_forward(t, q):
+        return pltpu.make_async_remote_copy(
+            src_ref=sig_slot(q), dst_ref=sig_slot(q), send_sem=sig_s.at[chips + t],
+            recv_sem=sig_r.at[q], device_id=other_core, device_id_type=MESH,
+        )
+
+    plane_start(sig_copy)
 
     def gram(lower):
         return jnp.where(mine, dot_t(lower, lower), 0.0)
@@ -149,8 +202,17 @@
     gram_one = gram(lower_one)
     gram_two = gram(lower_two)
 
-    each(pcols, lambda t: pltpu.make_async_copy(rx.at[t], rx.at[t], msg_r.at[t]).wait())
-    each(pcols, lambda t: pltpu.make_async_copy(par_rx.at[t], par_rx.at[t], par_r.at[t]).wait())
+    def tiles_wait(ref, sem):
+        pltpu.make_async_copy(ref, ref, sem).wait()
+
+    each(pcols, lambda t: tiles_wait(rx.at[t], msg_r.at[t]))
+    send_tiles(
+        [msg_two_copy, par_copy],
+        [
+            (msg.at[tiles:2 * tiles], rx_two.at[c], msg_two_r.at[c]),
+            (par_msg, par_rx.at[c], par_r.at[c]),
+        ],
+    )
 
     up = parent[j]
     rows_one = [pattern[j, k] for k in range(reach)]
@@ -171,25 +233,22 @@
     def fill(b):
         rows = pl.ds(pl.multiple_of(b * w, w), w)
         column, tile, hit = find(rows_one, None, b)
-        spread[rows, 0:w] = (rx[column, tile].astype(f32) * hit).astype(bf16)
+        spread_one[rows, :] = (rx[column, tile].astype(f32) * hit).astype(bf16)
+
+    def fill_two(b):
+        rows = pl.ds(pl.multiple_of(b * w, w), w)
         column, tile, hit = find(rows_two, kept, b)
-        spread[rows, w:2 * w] = (rx[column, tiles + tile].astype(f32) * hit).astype(bf16)
+        spread_two[rows, :] = (rx_two[column, tile].astype(f32) * hit).astype(bf16)
 
     each(tops, fill)
-    scaled_parent = jnp.concatenate(
-        [par_rx[t] for t in range(pcols)], axis=0
-    )
-
-    def sig_wait(t):
-        q, _ = peer(t)
-        ref = sig.at[q // pcols, pl.ds((q % pcols) * cols, cols)]
-        pltpu.make_async_copy(ref, ref, sig_r.at[q]).wait()
-
-    each(members, sig_wait, 1)
+    def sig_wait(q):
+        pltpu.make_async_copy(sig_slot(q), sig_slot(q), sig_r.at[q]).wait()
+
+    plane_wait(sig_wait, sig_forward)
 
     chunk = 8 if tops % 8 == 0 else 1
 
-    def product(b0):
+    def product(spread, b0):
         return [
             dot(
                 jnp.concatenate([sig[g, b0 + b] for b in range(chunk)], axis=1),
@@ -198,36 +257,42 @@
             for g in range(group)
         ]
 
-    if tops == chunk:
-        sums = product(0)
-    else:
+    def products(spread):
+        if tops == chunk:
+            return jnp.concatenate(product(spread, 0), axis=0)
         total[...] = jnp.zeros_like(total)
 
         def add(n):
-            for g, value in enumerate(product(n * chunk)):
+            for g, value in enumerate(product(spread, n * chunk)):
                 total[g] += value
 
         lax.fori_loop(0, tops // chunk, lambda n, carry: (add(n), carry)[1], 0)
-        sums = [total[g] for g in range(group)]
-
+        return jnp.concatenate([total[g] for g in range(group)], axis=0)
+
+    summed_one = products(spread_one)
     hits_one = [find(rows_one, None, z * group + g)[2] for g in range(group)]
     hits_two = [find(rows_two, kept, z * group + g)[2] for g in range(group)]
-    own_rows = spread[pl.ds(pl.multiple_of(z * group * w, w), group * w), :]
-    own_one, own_two = own_rows[:, 0:w], own_rows[:, w:2 * w]
-    summed_one = jnp.concatenate([s[:, 0:w] for s in sums], axis=0)
+    own = pl.ds(pl.multiple_of(z * group * w, w), group * w)
+    own_one = spread_one[own, :]
     for g in range(group):
-        ag[m, g] = (sums[g][:, 0:w] * -hits_one[g]).astype(bf16)
+        ag[m, g] = (summed_one[g * w:(g + 1) * w] * -hits_one[g]).astype(bf16)
     part_one = (gram_one + dot_t(own_one, summed_one.astype(bf16))).astype(bf16)
     ag[m, group] = part_one
     z_one[...] = part_one
 
-    def ag_copy(t):
+    def ag_copy(t, device):
         return pltpu.make_async_remote_copy(
             src_ref=ag.at[m], dst_ref=ag.at[m], send_sem=ag_s.at[t], recv_sem=ag_r.at[m],
-            device_id=peer(t)[1], device_id_type=MESH,
-        )
-
-    each(members, lambda t: ag_copy(t).start(), 1)
+            device_id=device, device_id_type=MESH,
+        )
+
+    def ag_forward(t, q):
+        return pltpu.make_async_remote_copy(
+            src_ref=ag.at[q], dst_ref=ag.at[q], send_sem=ag_s.at[chips + t],
+            recv_sem=ag_r.at[q], device_id=other_core, device_id_type=MESH,
+        )
+
+    plane_start(ag_copy)
 
     def z_copy(source, target, sem, recv):
         return pltpu.make_async_remote_copy(
@@ -242,11 +307,20 @@
     def _():
         first.start()
 
-    def ag_wait(t):
-        q, _ = peer(t)
+    def ag_wait(q):
         pltpu.make_async_copy(ag.at[q], ag.at[q], ag_r.at[q]).wait()
 
-    each(members, ag_wait, 1)
+    each(pcols, lambda t: tiles_wait(rx_two.at[t], msg_two_r.at[t]))
+    each(pcols, lambda t: tiles_wait(par_rx.at[t], par_r.at[t]))
+    each(tops, fill_two)
+    own_two = spread_two[own, :]
+    scaled_parent = jnp.concatenate(
+        [par_rx[t] for t in range(pcols)], axis=0
+    )
+
+    base_two = products(spread_two)
+
+    plane_wait(ag_wait, ag_forward)
 
     def out_one(row):
         return pltpu.make_async_copy(ag.at[place(row), x], top_one.at[0, row], store_s.at[row])
@@ -258,9 +332,7 @@
         slot = jnp.where(up == row, place(row), slot)
     inherited = jnp.concatenate([ag[slot, g] for g in range(group)], axis=0)
     up_diag = ag[slot, group]
-    summed_two = jnp.concatenate([s[:, w:2 * w] for s in sums], axis=0) + dot(
-        inherited, scaled_parent
-    )
+    summed_two = base_two + dot(inherited, scaled_parent)
     carried = dot_t(inherited, own_two) + dot(up_diag, scaled_parent)
     part_two = (
         gram_two
@@ -341,20 +413,21 @@
     each(tops, lambda row: out_two(row).wait())
     for copy in block_copies:
         copy.wait()
-    for copy_to in (msg_copy, par_copy):
+    for copy_to in (msg_copy, msg_two_copy, par_copy):
         each(planes, lambda t: copy_to(planes - t).wait_send(), 1)
 
     @pl.when(jnp.logical_not(stays))
     def _():
         msg_copy(0).wait_send()
+        msg_two_copy(0).wait_send()
         par_copy(0).wait_send()
 
     def drain(t):
-        sig_copy(t).wait_send()
-        ag_copy(t).wait_send()
         two_copy(t).wait_send()
 
     each(members, drain, 1)
+    plane_drain(sig_copy, sig_forward)
+    plane_drain(ag_copy, ag_forward)
 
     @pl.when(jnp.logical_not(mine))
     def _():
@@ -421,11 +494,13 @@
             pltpu.VMEM((3, w, w), f32),
             pltpu.VMEM((2 * tiles, w, w), bf16),
             pltpu.VMEM((w // pcols, w), bf16),
-            pltpu.VMEM((pcols, 2 * tiles, w, w), bf16),
+            pltpu.VMEM((pcols, tiles, w, w), bf16),
+            pltpu.VMEM((pcols, tiles, w, w), bf16),
             pltpu.VMEM((pcols, w // pcols, w), bf16),
             pltpu.VMEM((group, tops, w, w), bf16),
-            pltpu.VMEM((tops * w, 2 * w), bf16),
-            pltpu.VMEM((group, w, 2 * w), f32),
+            pltpu.VMEM((tops * w, w), bf16),
+            pltpu.VMEM((tops * w, w), bf16),
+            pltpu.VMEM((group, w, w), f32),
             pltpu.VMEM((members, group + 1, w, w), bf16),
             pltpu.VMEM((group, w, w), bf16),
             pltpu.VMEM((members, w, w), bf16),
@@ -434,7 +509,8 @@
             pltpu.VMEM((planes, w, w), bf16),
             pltpu.VMEM((planes, 2, w, w), bf16),
             pltpu.VMEM((3, w, w), bf16),
-            dma((planes,)), dma((planes,)), dma((pcols,)), dma((pcols,)),
+            dma((planes,)), dma((planes,)), dma((planes,)),
+            dma((pcols,)), dma((pcols,)), dma((pcols,)),
             dma((members,)), dma((members,)),
             dma((members,)), dma((members,)),
             dma((members,)), dma((members,)),

time: 40.3 us -> 35.9 us (0.89)
  Pallas kernels: 38.9 us -> 34.7 us
    pallas_call x1, Pallas kernels: 37.1 us -> 32.8 us  [body(): pl.pallas_call(functools.partial(kernel, prows, pcols, group), out_shape=...]
where the time goes in v4:
time: 35.9 us; the launch traced here: 35.4 us
  Pallas kernels  34.7 us (97%)
  between operations  0.64 us (2%)
    pallas_call x1, Pallas kernels, body(): pl.pallas_call(functools.partial(kernel, prows, pcols, group), out_shape=...  32.8 us
    pallas_call x1, Pallas kernels, body(): pl.pallas_call(write_out, out_shape=shapes, in_specs=[hbm] * 5, out_specs...  1.89 us

profile of v4, /device:TPU:0, one launch (start us, length us, event | category | flops | bytes accessed | tf_op | source)
XLA Modules:
  0.0 35.4 jit_solution(6434821228798160423)
XLA Ops:
  0.6 32.8 %shard_map.128 = (bf16[1,8,128,128]{3,2,1,0:T(8,128)(2,1)}, f32[1,128,128]{2,1,0:T(8,128)}, bf16[1,8,128,128]{3,2,1,0:T(8,128)(2,1)}, f32[1,128,128]{2,1,0:T(8,128)}, f32[1,128,128]{2,1,0:T(8,128)}) custom-call(bf16[1,2,128,128]{3,2,1,0:T(8,128)(2,1)} %sigma.1, bf16[1,2,128,128]{3,2,1,0:T(8,128)(2,1)} %factor_one_in.1, bf16[1,128,128]{2,1,0:T(8,128)(2,1)} %inverse_one_in.1, ...), custom_call_target="tpu_custom_call" | custom-call | tf_op jit(solution)/shard_map/pallas_call | solution.py:478
  33.5 1.9 %shard_map.129 = (bf16[1,8,128,128]{3,2,1,0:T(8,128)(2,1)}, f32[1,128,128]{2,1,0:T(8,128)}, bf16[1,8,128,128]{3,2,1,0:T(8,128)(2,1)}, f32[1,128,128]{2,1,0:T(8,128)}, f32[1,128,128]{2,1,0:T(8,128)}) custom-call(bf16[1,8,128,128]{3,2,1,0:T(8,128)(2,1)} %get-tuple-element.10.refs_0_, f32[1,128,128]{2,1,0:T(8,128)} %get-tuple-element.11.refs_1_, ...), custom_call_target="tpu_custom_call" | custom-call | tf_op jit(solution)/shard_map/pallas_call | solution.py:527

commit v5 on v4

--- a/solution.py
+++ b/solution.py
@@ -91,13 +91,15 @@
         each(chips, lambda t: copy(t, far(t)[1]).start(), 1)
         copy(0, other_core).start()
 
-    def plane_wait(wait, forward):
+    def plane_pass(wait, forward):
         def pass_on(t):
             q, _ = far(t)
             wait(q)
             forward(t, q).start()
 
         each(chips, pass_on, 1)
+
+    def plane_rest(wait):
         each(chips, lambda t: wait(near(t)))
 
     def plane_drain(copy, forward):
@@ -194,6 +196,9 @@
             recv_sem=sig_r.at[q], device_id=other_core, device_id_type=MESH,
         )
 
+    def sig_wait(q):
+        pltpu.make_async_copy(sig_slot(q), sig_slot(q), sig_r.at[q]).wait()
+
     plane_start(sig_copy)
 
     def gram(lower):
@@ -205,6 +210,7 @@
     def tiles_wait(ref, sem):
         pltpu.make_async_copy(ref, ref, sem).wait()
 
+    plane_pass(sig_wait, sig_forward)
     each(pcols, lambda t: tiles_wait(rx.at[t], msg_r.at[t]))
     send_tiles(
         [msg_two_copy, par_copy],
@@ -241,10 +247,7 @@
         spread_two[rows, :] = (rx_two[column, tile].astype(f32) * hit).astype(bf16)
 
     each(tops, fill)
-    def sig_wait(q):
-        pltpu.make_async_copy(sig_slot(q), sig_slot(q), sig_r.at[q]).wait()
-
-    plane_wait(sig_wait, sig_forward)
+    plane_rest(sig_wait)
 
     chunk = 8 if tops % 8 == 0 else 1
 
@@ -310,6 +313,8 @@
     def ag_wait(q):
         pltpu.make_async_copy(ag.at[q], ag.at[q], ag_r.at[q]).wait()
 
+    plane_pass(ag_wait, ag_forward)
+
     each(pcols, lambda t: tiles_wait(rx_two.at[t], msg_two_r.at[t]))
     each(pcols, lambda t: tiles_wait(par_rx.at[t], par_r.at[t]))
     each(tops, fill_two)
@@ -320,7 +325,7 @@
 
     base_two = products(spread_two)
 
-    plane_wait(ag_wait, ag_forward)
+    plane_rest(ag_wait)
 
     def out_one(row):
         return pltpu.make_async_copy(ag.at[place(row), x], top_one.at[0, row], store_s.at[row])

time: 35.9 us -> 36.5 us (1.017)
  Pallas kernels: 34.7 us -> 35.4 us
    pallas_call x1, Pallas kernels: 32.8 us -> 33.5 us  [body(): pl.pallas_call(functools.partial(kernel, prows, pcols, group), out_shape=...]
where the time goes in v5:
time: 36.5 us; the launch traced here: 36 us
  Pallas kernels  35.4 us (97%)
  between operations  0.64 us (2%)
    pallas_call x1, Pallas kernels, body(): pl.pallas_call(functools.partial(kernel, prows, pcols, group), out_shape=...  33.5 us
    pallas_call x1, Pallas kernels, body(): pl.pallas_call(write_out, out_shape=shapes, in_specs=[hbm] * 5, out_specs...  1.89 us

profile of v5, /device:TPU:0, one launch (start us, length us, event | category | flops | bytes accessed | tf_op | source)
XLA Modules:
  0.0 36.0 jit_solution(15723292706801529974)
XLA Ops:
  0.6 33.5 %shard_map.128 = (bf16[1,8,128,128]{3,2,1,0:T(8,128)(2,1)}, f32[1,128,128]{2,1,0:T(8,128)}, bf16[1,8,128,128]{3,2,1,0:T(8,128)(2,1)}, f32[1,128,128]{2,1,0:T(8,128)}, f32[1,128,128]{2,1,0:T(8,128)}) custom-call(bf16[1,2,128,128]{3,2,1,0:T(8,128)(2,1)} %sigma.1, bf16[1,2,128,128]{3,2,1,0:T(8,128)(2,1)} %factor_one_in.1, bf16[1,128,128]{2,1,0:T(8,128)(2,1)} %inverse_one_in.1, ...), custom_call_target="tpu_custom_call" | custom-call | tf_op jit(solution)/shard_map/pallas_call | solution.py:483
  34.1 1.9 %shard_map.129 = (bf16[1,8,128,128]{3,2,1,0:T(8,128)(2,1)}, f32[1,128,128]{2,1,0:T(8,128)}, bf16[1,8,128,128]{3,2,1,0:T(8,128)(2,1)}, f32[1,128,128]{2,1,0:T(8,128)}, f32[1,128,128]{2,1,0:T(8,128)}) custom-call(bf16[1,8,128,128]{3,2,1,0:T(8,128)(2,1)} %get-tuple-element.10.refs_0_, f32[1,128,128]{2,1,0:T(8,128)} %get-tuple-element.11.refs_1_, ...), custom_call_target="tpu_custom_call" | custom-call | tf_op jit(solution)/shard_map/pallas_call | solution.py:532
